TPU v7x, 32 devices: a whole 2x2x4 slice. The times are simulated.
32 devices in a mesh: groups: 2 (over y), ctx: 4 (over z), exp: 2 (over x), head: 2 (over core).
Axes of the slice: x: 2, y: 2, z: 4, core: 2. Of those that a mesh axis runs over, the one named last changes fastest.
Arguments:
- latent: bfloat16 [256, 576], P(('groups', 'ctx')), parts along dimension 0, may hold values from -5 to 5
- query: bfloat16 [256, 3072], P(('groups', 'ctx'), ('exp', 'head')), parts along dimension 0, may hold values from -30 to 30
- w_uk: bfloat16 [512, 2048], P(None, ('exp', 'head')), may hold values from -0.25 to 0.25
- w_uv: bfloat16 [512, 2048], P(None, ('exp', 'head')), may hold values from -0.25 to 0.25
- w_o: bfloat16 [2048, 3584], P(('exp', 'head'), 'ctx'), may hold values from -0.5 to 0.5
- resid: bfloat16 [256, 3584], P(('groups', 'ctx', 'exp', 'head')), parts along dimension 0, may hold values from -6 to 6
- norm_gain: float32 [3584], replicated, may hold values from 0.1 to 1.9
- w_gate: bfloat16 [4, 3584, 2048], P(('exp', 'head'), None, 'ctx'), may hold values from -0.09375 to 0.09375
- w_up: bfloat16 [4, 3584, 2048], P(('exp', 'head'), None, 'ctx'), may hold values from -0.09375 to 0.09375
- w_down: bfloat16 [4, 2048, 3584], P(('exp', 'head'), None, 'ctx'), may hold values from -0.125 to 0.125
- expert_ids: int32 [256, 2], P(('groups', 'ctx', 'exp', 'head')), parts along dimension 0, may hold values from 0 to 3, all different within a row; in each aligned block of 8 rows (0 to 7, 8 to 15, ...) at most 8 rows name the same one
- route_weights: float32 [256, 2], P(('groups', 'ctx', 'exp', 'head')), parts along dimension 0, may hold values from 0.2 to 1
Outputs:
- layer_out: bfloat16 [256, 3584], P(('groups', 'ctx', 'exp', 'head')), parts along dimension 0
There are 2 independent parts, one for each index of `groups`. A program takes and returns all parts, laid end to end along the dimension named above; an argument that names none is the same for every part. Nothing has to cross between parts.
Inputs may be any that keep to these rules, and one draw needn't show every extreme that they name: `expert_ids`: each token names 2 different experts; within each aligned block of 8 tokens no expert is named more than 8 times, a bound that some block reaches.
All inputs are finite; a program needn't handle non-finite values.
Results may differ from a plain program's by a relative error of at most 0.014.
Values may be sent and summed in bfloat16 or wider, within the bound.
A program may use at most 64 MiB of HBM per device.

v0:
```python
import math
import jax
import jax.numpy as jnp
from jax import lax
from jax.sharding import PartitionSpec as P

D = 3584
NOPE = 128
ROPE = 64
LATENT = 512


def shards(
    latent,
    query,
    w_uk,
    w_uv,
    w_o,
    resid,
    norm_gain,
    w_gate,
    w_up,
    w_down,
    expert_ids,
    route_weights,
):
    qblock = query.shape[0]
    head_width = NOPE + ROPE
    heads_here = query.shape[1] // head_width
    nope_span = heads_here * NOPE
    score_scale = 1.0 / math.sqrt(head_width)
    query_all = query.reshape(qblock, heads_here, head_width)
    query_nope = query_all[:, :, :NOPE]
    query_rope = query_all[:, :, NOPE:]
    query_pos = lax.axis_index("ctx") * qblock + jnp.arange(qblock, dtype=jnp.int32)
    shard_rows = lax.all_gather(latent, "ctx", axis=0, tiled=True)
    piece_rows = shard_rows.shape[0]
    compressed = shard_rows[:, :LATENT]
    key_nope = (
        jnp.dot(compressed, w_uk, preferred_element_type=jnp.float32)
        .astype(jnp.bfloat16)
        .reshape(piece_rows, heads_here, NOPE)
    )
    values = (
        jnp.dot(compressed, w_uv, preferred_element_type=jnp.float32)
        .astype(jnp.bfloat16)
        .reshape(piece_rows, heads_here, NOPE)
    )
    run_max = jnp.full((qblock, heads_here), -1e30, jnp.float32)
    piece_rows = key_nope.shape[0]
    scores = jnp.einsum("qhd,khd->qhk", query_nope, key_nope, preferred_element_type=jnp.float32)
    scores = (
        scores
        + jnp.einsum(
            "qhd,kd->qhk", query_rope, shard_rows[:, LATENT:], preferred_element_type=jnp.float32
        )
    ) * score_scale
    key_pos = jnp.arange(piece_rows, dtype=jnp.int32)
    allowed = (key_pos[None, :] <= query_pos[:, None])[:, None, :]
    new_max = jnp.maximum(run_max, jnp.max(jnp.where(allowed, scores, -1e30), axis=2))
    exponent = jnp.where(allowed, jnp.exp(scores - new_max[:, :, None]), 0.0)
    run_sum = jnp.sum(exponent, axis=2)
    weighted_sum = jnp.einsum(
        "qhk,khd->qhd", exponent.astype(jnp.bfloat16), values, preferred_element_type=jnp.float32
    )
    attn_state = (new_max, run_sum, weighted_sum)
    run_max, run_sum, weighted_sum = attn_state
    attended = (weighted_sum / run_sum[:, :, None]).astype(jnp.bfloat16).reshape(qblock, nope_span)
    tok_dev = resid.shape[0]
    ctx_count = lax.axis_size("ctx")
    partial_value = jnp.dot(
        lax.all_gather(attended, "ctx", axis=0, tiled=True), w_o, preferred_element_type=jnp.float32
    )
    partial_value = partial_value.astype(jnp.bfloat16).reshape(ctx_count, qblock, w_o.shape[1])
    summed = lax.psum_scatter(
        partial_value, ("exp", "head"), scatter_dimension=1, tiled=True
    ).astype(jnp.float32)
    swapped = lax.all_to_all(
        summed.astype(jnp.bfloat16), "ctx", split_axis=0, concat_axis=2, tiled=True
    ).astype(summed.dtype)
    projected = swapped.reshape(tok_dev, D)
    residual_sum = resid.astype(jnp.float32) + projected
    inverse_rms = lax.rsqrt(jnp.mean(residual_sum * residual_sum, axis=1, keepdims=True) + 1e-06)
    normalized = (residual_sum * inverse_rms * norm_gain).astype(jnp.bfloat16)
    experts = lax.axis_size(("exp", "head"))
    top_count = expert_ids.shape[1]
    capacity = max(2, 2 * tok_dev * top_count // experts)
    flat_ids = expert_ids.reshape(-1)
    onehot = (flat_ids[:, None] == jnp.arange(experts, dtype=jnp.int32)[None, :]).astype(jnp.int32)
    slot_rank = jnp.sum((jnp.cumsum(onehot, axis=0) - onehot) * onehot, axis=1)
    target = (flat_ids * capacity + slot_rank).reshape(tok_dev, top_count)
    slot_ids = jnp.arange(experts * capacity, dtype=jnp.int32)
    route_hits = (target[:, :, None] == slot_ids[None, None, :]).astype(jnp.float32)
    picker = jnp.sum(route_hits, axis=1).astype(jnp.bfloat16)
    dispatched = jnp.einsum(
        "ts,td->sd", picker, normalized, preferred_element_type=jnp.float32
    ).astype(jnp.bfloat16)
    outgoing = dispatched.reshape(experts, capacity, D)
    arrived = lax.all_to_all(outgoing, ("exp", "head"), split_axis=0, concat_axis=0, tiled=True)
    rows_in = arrived.reshape(experts * capacity, D)
    gate_local = w_gate[0]
    up_local = w_up[0]
    down_local = w_down[0]
    shard_rows = lax.all_gather(rows_in, "ctx", axis=0, tiled=True)
    gate_part = jnp.dot(shard_rows, gate_local, preferred_element_type=jnp.float32)
    up_part = jnp.dot(shard_rows, up_local, preferred_element_type=jnp.float32)
    hidden_cols = (jax.nn.silu(gate_part) * up_part).astype(jnp.bfloat16)
    expert_cols = jnp.dot(
        lax.all_gather(hidden_cols, "ctx", axis=1, tiled=True),
        down_local,
        preferred_element_type=jnp.float32,
    ).astype(jnp.bfloat16)
    returned = lax.all_to_all(
        expert_cols.reshape(ctx_count, experts * capacity, down_local.shape[1]),
        "ctx",
        split_axis=0,
        concat_axis=2,
        tiled=True,
    )
    returned_rows = lax.all_to_all(
        returned.reshape(experts, capacity, D),
        ("exp", "head"),
        split_axis=0,
        concat_axis=0,
        tiled=True,
    )
    returned_rows = returned_rows.reshape(experts * capacity, D)
    weighted = jnp.sum(route_hits * route_weights[:, :, None], axis=1)
    moe_sum = jnp.dot(weighted, returned_rows.astype(jnp.float32), precision=lax.Precision.HIGHEST)
    return (residual_sum + moe_sum).astype(jnp.bfloat16)


def solution(mesh):
    placed = (
        P(("groups", "ctx"), None),
        P(("groups", "ctx"), ("exp", "head")),
        P(None, ("exp", "head")),
        P(None, ("exp", "head")),
        P(("exp", "head"), "ctx"),
        P(("groups", "ctx", "exp", "head"), None),
        P(),
        P(("exp", "head"), None, "ctx"),
        P(("exp", "head"), None, "ctx"),
        P(("exp", "head"), None, "ctx"),
        P(("groups", "ctx", "exp", "head"), None),
        P(("groups", "ctx", "exp", "head"), None),
    )
    return jax.shard_map(
        shards,
        mesh=mesh,
        in_specs=placed,
        out_specs=P(("groups", "ctx", "exp", "head"), None),
        check_vma=False,
    )
```

profile of v0, /device:TPU:0, one launch (start us, length us, event | category | flops | bytes accessed | tf_op | source)
XLA Modules:
  0.0 148.8 jit_solution(2626256943590443223)
XLA Ops:
  6.5 0.0 copy-start
  6.5 0.0 copy-start.4
  6.5 0.0 copy-start.5
  6.5 0.0 copy-start.2
  6.5 0.0 copy-start.3
  6.5 0.0 reduce-scatter.4.cloned.1.call-start
  6.6 1.0 reshape.85
  7.6 0.1 iota_compare_fusion
  7.7 15.4 %all_gather.12 = bf16[128,576]{1,0:T(8,128)(2,1)S(1)} all-gather(bf16[32,576]{1,0:T(8,128)(2,1)} %param.12), channel_id=1, replica_groups=mesh['groups'=2,'ctx'=4,'exp'=2,'head'=2] {'ctx'}, dimensions={0}, use_global_device_ids=true | all-gather | bytes 184320 | tf_op jit(solution)/shard_map/all_gather | solution.py:36
  23.1 1.3 fusion.19
  24.4 1.3 fusion.18
  25.7 0.2 convolution_bitcast_fusion.1
  25.8 0.3 select_reduce_fusion
  26.1 0.2 convolution_bitcast_fusion
  26.3 0.3 fusion.23
  26.7 13.5 %all_gather.13 = bf16[128,512]{1,0:T(8,128)(2,1)S(1)} all-gather(bf16[32,512]{1,0:T(8,128)(2,1)S(1)} %bitcast.80), channel_id=1, replica_groups=mesh['groups'=2,'ctx'=4,'exp'=2,'head'=2] {'ctx'}, dimensions={0}, use_global_device_ids=true | all-gather | bytes 163840 | tf_op jit(solution)/shard_map/all_gather | solution.py:72
  40.2 0.0 copy-done
  40.2 0.3 convolution_convert_fusion.1
  40.5 0.1 copy.49
  40.6 0.7 copy.57
  41.3 0.0 reduce-scatter.4.cloned.1.call-update
  41.4 0.0 copy-done.4
  41.4 0.1 copy.45
  41.5 0.1 eq.28
  41.5 0.1 fusion.44
  41.6 0.2 select_reduce_fusion.2
  41.8 0.1 reduce_sum.49
  41.9 0.1 copy.47
  42.0 20.8 %reduce-scatter.4.cloned.1.call-done = bf16[8,3584]{1,0:T(8,128)(2,1)} async-done(((bf16[32,3584]{1,0:T(8,128)(2,1)}), bf16[8,3584]{1,0:T(8,128)(2,1)}) %reduce-scatter.4.cloned.1.call-update) | async-done | bytes 57360
  62.8 0.8 reshape.97
  63.6 0.6 copy.50
  64.3 4.6 %all-to-all-start = ((bf16[4,8,896]{2,1,0:T(8,128)(2,1)}), bf16[4,8,896]{2,1,0:T(8,128)(2,1)S(1)}, u32[]{:S(2)}, u32[]{:S(2)}) async-start(bf16[4,8,896]{2,1,0:T(8,128)(2,1)} %copy.50), calls=%async_computation | async-start | bytes 114688 | tf_op jit(solution)/shard_map/all_to_all | solution.py:78
  68.9 0.0 copy-done.5
  68.9 0.1 convert_reduce_fusion
  68.9 5.6 %all-to-all-done = bf16[4,8,896]{2,1,0:T(8,128)(2,1)S(1)} async-done(((bf16[4,8,896]{2,1,0:T(8,128)(2,1)}), bf16[4,8,896]{2,1,0:T(8,128)(2,1)S(1)}, u32[]{:S(2)}, u32[]{:S(2)}) %all-to-all-start) | async-done | bytes 57376 | tf_op jit(solution)/shard_map/all_to_all | solution.py:78
  74.6 0.0 copy-start.6
  74.6 0.0 copy-done.2
  74.6 0.1 multiply_reduce_fusion
  74.8 0.0 copy-done.3
  74.8 0.3 fusion.1
  75.0 8.2 %all_to_all.34 = bf16[4,8,3584]{2,1,0:T(8,128)(2,1)S(1)} all-to-all(bf16[4,8,3584]{2,1,0:T(8,128)(2,1)S(1)} %fusion.1), channel_id=1, replica_groups=mesh['groups'=2,'ctx'=4,'exp'=2,'head'=2] {'exp','head'}, dimensions={0} | all-to-all | bytes 458752 | tf_op jit(solution)/shard_map/all_to_all | solution.py:99
  83.2 19.1 %all_gather.14 = bf16[128,3584]{1,0:T(8,128)(2,1)S(1)} all-gather(bf16[32,3584]{1,0:T(8,128)(2,1)S(1)} %bitcast.77), channel_id=1, replica_groups=mesh['groups'=2,'ctx'=4,'exp'=2,'head'=2] {'ctx'}, dimensions={0}, use_global_device_ids=true | all-gather | bytes 1146880 | tf_op jit(solution)/shard_map/all_gather | solution.py:104
  102.3 2.7 %fusion.7 = f32[128,512]{1,0:T(8,128)S(1)} fusion(bf16[128,3584]{1,0:T(8,128)(2,1)S(1)} %all_gather.14, bf16[1,3584,512]{2,1,0:T(8,128)(2,1)} %param.19), kind=kOutput, calls=%fused_computation.9 | convolution fusion | flops 469762048 | bytes 4849664 | tf_op jit(solution)/shard_map/dot_general | solution.py:105
  104.9 0.0 copy-done.6
  105.0 0.0 copy-start.1
  105.0 0.6 fusion.15
  105.6 15.8 %all_gather.15 = bf16[128,2048]{1,0:T(8,128)(2,1)S(1)} all-gather(bf16[128,512]{1,0:T(8,128)(2,1)S(1)} %fusion.15), channel_id=1, replica_groups=mesh['groups'=2,'ctx'=4,'exp'=2,'head'=2] {'ctx'}, dimensions={1}, use_global_device_ids=true | all-gather | bytes 655360 | tf_op jit(solution)/shard_map/all_gather | solution.py:109
  121.4 0.0 copy-done.1
  121.4 0.7 fusion.9
  122.1 10.7 %all_to_all.35 = bf16[4,32,896]{2,1,0:T(8,128)(2,1)S(1)} all-to-all(bf16[4,32,896]{2,1,0:T(8,128)(2,1)S(1)} %bitcast.78), channel_id=1, replica_groups=mesh['groups'=2,'ctx'=4,'exp'=2,'head'=2] {'ctx'}, dimensions={0} | all-to-all | bytes 458752 | tf_op jit(solution)/shard_map/all_to_all | solution.py:113
  132.9 0.1 copy.48
  133.0 0.1 reshape.91
  133.1 8.0 %all_to_all.36 = bf16[4,8,3584]{2,1,0:T(8,128)(2,1)S(1)} all-to-all(bf16[4,8,3584]{2,1,0:T(8,128)(2,1)S(1)} %reshape.91), channel_id=1, replica_groups=mesh['groups'=2,'ctx'=4,'exp'=2,'head'=2] {'exp','head'}, dimensions={0} | all-to-all | bytes 458752 | tf_op jit(solution)/shard_map/all_to_all | solution.py:120
  141.1 0.8 fusion.2
  (9 shorter events, 0.1 us)
Async XLA Ops:
  6.5 33.7 %copy-start = (bf16[512,896]{1,0:T(8,128)(2,1)S(1)}, bf16[512,896]{1,0:T(8,128)(2,1)}, u32[]{:S(2)}) copy-start(bf16[512,896]{1,0:T(8,128)(2,1)} %param.16) | copy-start | bytes 2752516
  6.5 34.8 %copy-start.4 = (s32[8,2]{0,1:T(2,128)S(1)}, s32[8,2]{0,1:T(2,128)}, u32[]{:S(2)}) copy-start(s32[8,2]{0,1:T(2,128)} %param.22) | copy-start | bytes 196
  6.5 62.3 %copy-start.5 = (f32[8,2]{0,1:T(2,128)S(1)}, f32[8,2]{0,1:T(2,128)}, u32[]{:S(2)}) copy-start(f32[8,2]{0,1:T(2,128)} %param.23) | copy-start | bytes 196
  6.5 68.1 %copy-start.2 = (bf16[8,3584]{1,0:T(8,128)(2,1)S(1)}, bf16[8,3584]{1,0:T(8,128)(2,1)}, u32[]{:S(2)}) copy-start(bf16[8,3584]{1,0:T(8,128)(2,1)} %param.17) | copy-start | bytes 172036
  6.5 68.2 %copy-start.3 = (f32[3584]{0:T(1024)S(1)}, f32[3584]{0:T(1024)}, u32[]{:S(2)}) copy-start(f32[3584]{0:T(1024)} %param.18) | copy-start | bytes 43012
  6.5 56.2 %reduce-scatter.4.cloned.1.call-start = ((), (), s32[]{:S(2)}) async-start(), calls=%async_computation.5 | async-start | bytes 286720
  64.3 10.3 %all-to-all-start = ((bf16[4,8,896]{2,1,0:T(8,128)(2,1)}), bf16[4,8,896]{2,1,0:T(8,128)(2,1)S(1)}, u32[]{:S(2)}, u32[]{:S(2)}) async-start(bf16[4,8,896]{2,1,0:T(8,128)(2,1)} %copy.50), calls=%async_computation | async-start | bytes 114688 | tf_op jit(solution)/shard_map/all_to_all | solution.py:78
  74.6 30.4 %copy-start.6 = (bf16[1,3584,512]{2,1,0:T(8,128)(2,1)S(1)}, bf16[1,3584,512]{2,1,0:T(8,128)(2,1)}, u32[]{:S(2)}) copy-start(bf16[1,3584,512]{2,1,0:T(8,128)(2,1)} %param.20) | copy-start | bytes 11010052
  105.0 16.4 %copy-start.1 = (bf16[1,2048,896]{2,1,0:T(8,128)(2,1)S(1)}, bf16[1,2048,896]{2,1,0:T(8,128)(2,1)}, u32[]{:S(2)}) copy-start(bf16[1,2048,896]{2,1,0:T(8,128)(2,1)} %param.21) | copy-start | bytes 11010052
Sparse Core Ops, SparseCore 0:
  41.5 21.2 reduce-scatter.3
where the time goes:
time: 149 us
  blocking collectives  90.6 us (61%)
  waiting for transfers between devices  26.4 us (18%)
  between operations  13.6 us (9%)
  matrix products  8.65 us (6%)
  starting transfers between devices  4.63 us (3%)
  local copies, waits for them, and re-layouts  3.88 us (3%)
    unnamed x2, waiting for transfers between devices  20.8 us
    all_gather x1, blocking collectives, shards(): shard_rows = lax.all_gather(rows_in, 'ctx', axis=0, tiled=True)  19.1 us
    all_gather x1, blocking collectives, shards(): lax.all_gather(hidden_cols, 'ctx', axis=1, tiled=True)  15.8 us
    all_gather x1, blocking collectives, shards(): shard_rows = lax.all_gather(latent, 'ctx', axis=0, tiled=True)  15.4 us
    all_gather x1, blocking collectives, shards(): lax.all_gather(attended, 'ctx', axis=0, tiled=True)  13.5 us
    all_to_all x1, blocking collectives, shards(): lax.all_to_all(expert_cols.reshape(ctx_count, experts * capacity, down_lo...  10.7 us
    all_to_all x1, blocking collectives, shards(): lax.all_to_all(outgoing, ('exp', 'head'), split_axis=0, concat_axis=0, ti...  8.16 us
    all_to_all x1, blocking collectives, shards(): lax.all_to_all(returned.reshape(experts, capacity, D), ('exp', 'head'), s...  8.03 us
  transfers between devices with their start and end apart: 2, of which 2 were waited for; matrix products, arithmetic and copies ran while one was open for 0% of the time, Pallas kernels for 0%

commit v1 on v0

--- a/solution.py
+++ b/solution.py
@@ -33,7 +33,13 @@
     query_nope = query_all[:, :, :NOPE]
     query_rope = query_all[:, :, NOPE:]
     query_pos = lax.axis_index("ctx") * qblock + jnp.arange(qblock, dtype=jnp.int32)
-    shard_rows = lax.all_gather(latent, "ctx", axis=0, tiled=True)
+    size = lax.axis_size("ctx")
+    moving, shards_2 = (latent, [latent])
+    for _ in range(size - 1):
+        moving = lax.ppermute(moving, "ctx", [(i, (i + 1) % size) for i in range(size)])
+        shards_2.insert(0, moving)
+    line = jnp.concatenate(shards_2, axis=0)
+    shard_rows = jnp.roll(line, (lax.axis_index("ctx") + 1) * latent.shape[0], axis=0)
     piece_rows = shard_rows.shape[0]
     compressed = shard_rows[:, :LATENT]
     key_nope = (

time: 149 us -> 154 us (1.034)
  blocking collectives: 90.6 us -> 75.1 us
  waiting for transfers between devices: 26.4 us -> 41.4 us
  starting transfers between devices: 4.63 us -> 7.71 us
  local copies, waits for them, and re-layouts: 3.88 us -> 6.03 us
    ppermute x0 -> x3, waiting for transfers between devices: none -> 17.8 us  [shards(): lax.ppermute(moving, 'ctx', [(i, (i + 1) % size) for i in range(size)])]
    all_gather x1 -> x0, blocking collectives: 15.4 us -> none  [shards(): shard_rows = lax.all_gather(latent, 'ctx', axis=0, tiled=True)]
    ppermute x0 -> x3, starting transfers between devices: none -> 3.11 us  [shards(): lax.ppermute(moving, 'ctx', [(i, (i + 1) % size) for i in range(size)])]
    unnamed x2, waiting for transfers between devices: 20.8 us -> 17.9 us
    unnamed x19 -> x18, local copies, waits for them, and re-layouts: 2.4 us -> 4.07 us
  transfers between devices with their start and end apart: 2 -> 5, of which waited for: 2 -> 5; matrix products, arithmetic and copies ran while one was open for 0% -> 2% of each run, Pallas kernels for 0% -> 0%
where the time goes in v1:
time: 154 us
  blocking collectives  75.1 us (49%)
  waiting for transfers between devices  41.4 us (27%)
  between operations  13.6 us (9%)
  matrix products  8.93 us (6%)
  starting transfers between devices  7.71 us (5%)
  local copies, waits for them, and re-layouts  6.03 us (4%)
    all_gather x1, blocking collectives, shards(): shard_rows = lax.all_gather(rows_in, 'ctx', axis=0, tiled=True)  19.1 us
    unnamed x2, waiting for transfers between devices  17.9 us
    ppermute x3, waiting for transfers between devices, shards(): lax.ppermute(moving, 'ctx', [(i, (i + 1) % size) for i in range(size)])  17.8 us
    all_gather x1, blocking collectives, shards(): lax.all_gather(hidden_cols, 'ctx', axis=1, tiled=True)  15.8 us
    all_gather x1, blocking collectives, shards(): lax.all_gather(attended, 'ctx', axis=0, tiled=True)  13.4 us
    all_to_all x1, blocking collectives, shards(): lax.all_to_all(expert_cols.reshape(ctx_count, experts * capacity, down_lo...  10.7 us
    all_to_all x1, blocking collectives, shards(): lax.all_to_all(outgoing, ('exp', 'head'), split_axis=0, concat_axis=0, ti...  8.16 us
    all_to_all x1, blocking collectives, shards(): lax.all_to_all(returned.reshape(experts, capacity, D), ('exp', 'head'), s...  8.03 us
  transfers between devices with their start and end apart: 5, of which 5 were waited for; matrix products, arithmetic and copies ran while one was open for 2% of the time, Pallas kernels for 0%

profile of v1, /device:TPU:0, one launch (start us, length us, event | category | flops | bytes accessed | tf_op | source)
XLA Modules:
  0.0 153.7 jit_solution(5579182870765269741)
XLA Ops:
  6.5 0.0 copy-start
  6.5 0.0 reduce-scatter.4.cloned.1.call-start
  6.5 1.0 copy.45
  7.5 3.1 %collective-permute-start = (bf16[32,576]{0,1:T(8,128)(2,1)S(1)}, bf16[32,576]{0,1:T(8,128)(2,1)S(1)}, u32[]{:S(2)}, u32[]{:S(2)}) collective-permute-start(bf16[32,576]{0,1:T(8,128)(2,1)S(1)} %copy.45), channel_id=1, source_target_pairs={{0,4},{4,8},{8,12},{12,0},{1,5},{5,9},{9,13},{13,1},{2,6},{6,10},{... | collective-permute-start | bytes 110600 | tf_op jit(solution)/shard_map/ppermute | solution.py:39
  10.6 5.9 %collective-permute-done = bf16[32,576]{0,1:T(8,128)(2,1)S(1)} collective-permute-done((bf16[32,576]{0,1:T(8,128)(2,1)S(1)}, bf16[32,576]{0,1:T(8,128)(2,1)S(1)}, u32[]{:S(2)}, u32[]{:S(2)}) %collective-permute-start) | collective-permute-done | bytes 36896 | tf_op jit(solution)/shard_map/ppermute | solution.py:39
  16.5 0.0 collective-permute-start.1
  16.5 6.9 %collective-permute-done.1 = bf16[32,576]{0,1:T(8,128)(2,1)S(1)} collective-permute-done((bf16[32,576]{0,1:T(8,128)(2,1)S(1)}, bf16[32,576]{0,1:T(8,128)(2,1)S(1)}, u32[]{:S(2)}, u32[]{:S(2)}) %collective-permute-start.1) | collective-permute-done | bytes 36896 | tf_op jit(solution)/shard_map/ppermute | solution.py:39
  23.5 0.0 collective-permute-start.2
  23.5 0.1 iota_compare_fusion
  23.5 0.0 copy-start.4
  23.5 0.9 reshape.85
  24.5 0.0 copy-start.2
  24.5 0.8 copy.53
  25.3 0.1 eq.31
  25.4 0.0 copy-start.3
  25.4 5.0 %collective-permute-done.2 = bf16[32,576]{0,1:T(8,128)(2,1)S(1)} collective-permute-done((bf16[32,576]{0,1:T(8,128)(2,1)S(1)}, bf16[32,576]{0,1:T(8,128)(2,1)S(1)}, u32[]{:S(2)}, u32[]{:S(2)}) %collective-permute-start.2) | collective-permute-done | bytes 36896 | tf_op jit(solution)/shard_map/ppermute | solution.py:39
  30.4 0.5 concatenate.6
  30.9 1.4 fusion.19
  32.3 1.4 fusion.18
  33.7 0.2 convolution_bitcast_fusion.2
  33.9 0.3 select_reduce_fusion
  34.2 0.2 convolution_bitcast_fusion
  34.4 0.3 fusion.24
  34.8 13.4 %all_gather.9 = bf16[128,512]{1,0:T(8,128)(2,1)S(1)} all-gather(bf16[32,512]{1,0:T(8,128)(2,1)S(1)} %bitcast.85), channel_id=1, replica_groups=mesh['groups'=2,'ctx'=4,'exp'=2,'head'=2] {'ctx'}, dimensions={0}, use_global_device_ids=true | all-gather | bytes 163840 | tf_op jit(solution)/shard_map/all_gather | solution.py:78
  48.1 0.0 copy-done
  48.2 0.3 convolution_convert_fusion.1
  48.5 0.1 copy.57
  48.6 0.7 copy.64
  49.3 0.0 reduce-scatter.4.cloned.1.call-update
  49.3 0.1 fusion.45
  49.4 0.2 select_reduce_fusion.2
  49.6 0.1 reduce_sum.49
  49.7 0.1 copy.55
  49.8 17.9 %reduce-scatter.4.cloned.1.call-done = bf16[8,3584]{1,0:T(8,128)(2,1)} async-done(((bf16[32,3584]{1,0:T(8,128)(2,1)}), bf16[8,3584]{1,0:T(8,128)(2,1)}) %reduce-scatter.4.cloned.1.call-update) | async-done | bytes 57360
  67.7 0.8 reshape.97
  68.5 0.6 copy.58
  69.1 4.6 %all-to-all-start = ((bf16[4,8,896]{2,1,0:T(8,128)(2,1)}), bf16[4,8,896]{2,1,0:T(8,128)(2,1)S(1)}, u32[]{:S(2)}, u32[]{:S(2)}) async-start(bf16[4,8,896]{2,1,0:T(8,128)(2,1)} %copy.58), calls=%async_computation | async-start | bytes 114688 | tf_op jit(solution)/shard_map/all_to_all | solution.py:84
  73.7 0.0 copy-done.4
  73.7 0.1 convert_reduce_fusion
  73.8 5.6 %all-to-all-done = bf16[4,8,896]{2,1,0:T(8,128)(2,1)S(1)} async-done(((bf16[4,8,896]{2,1,0:T(8,128)(2,1)}), bf16[4,8,896]{2,1,0:T(8,128)(2,1)S(1)}, u32[]{:S(2)}, u32[]{:S(2)}) %all-to-all-start) | async-done | bytes 57376 | tf_op jit(solution)/shard_map/all_to_all | solution.py:84
  79.5 0.0 copy-start.5
  79.5 0.0 copy-done.2
  79.5 0.1 multiply_reduce_fusion
  79.6 0.0 copy-done.3
  79.7 0.3 fusion.1
  79.9 8.2 %all_to_all.34 = bf16[4,8,3584]{2,1,0:T(8,128)(2,1)S(1)} all-to-all(bf16[4,8,3584]{2,1,0:T(8,128)(2,1)S(1)} %fusion.1), channel_id=1, replica_groups=mesh['groups'=2,'ctx'=4,'exp'=2,'head'=2] {'exp','head'}, dimensions={0} | all-to-all | bytes 458752 | tf_op jit(solution)/shard_map/all_to_all | solution.py:105
  88.1 19.1 %all_gather.10 = bf16[128,3584]{1,0:T(8,128)(2,1)S(1)} all-gather(bf16[32,3584]{1,0:T(8,128)(2,1)S(1)} %bitcast.82), channel_id=1, replica_groups=mesh['groups'=2,'ctx'=4,'exp'=2,'head'=2] {'ctx'}, dimensions={0}, use_global_device_ids=true | all-gather | bytes 1146880 | tf_op jit(solution)/shard_map/all_gather | solution.py:110
  107.1 2.7 %fusion.7 = f32[128,512]{1,0:T(8,128)S(1)} fusion(bf16[128,3584]{1,0:T(8,128)(2,1)S(1)} %all_gather.10, bf16[1,3584,512]{2,1,0:T(8,128)(2,1)} %param.19), kind=kOutput, calls=%fused_computation.9 | convolution fusion | flops 469762048 | bytes 4849664 | tf_op jit(solution)/shard_map/dot_general | solution.py:111
  109.8 0.0 copy-done.5
  109.8 0.0 copy-start.1
  109.8 0.7 fusion.15
  110.5 15.8 %all_gather.11 = bf16[128,2048]{1,0:T(8,128)(2,1)S(1)} all-gather(bf16[128,512]{1,0:T(8,128)(2,1)S(1)} %fusion.15), channel_id=1, replica_groups=mesh['groups'=2,'ctx'=4,'exp'=2,'head'=2] {'ctx'}, dimensions={1}, use_global_device_ids=true | all-gather | bytes 655360 | tf_op jit(solution)/shard_map/all_gather | solution.py:115
  126.3 0.0 copy-done.1
  126.3 0.7 fusion.9
  127.0 10.7 %all_to_all.35 = bf16[4,32,896]{2,1,0:T(8,128)(2,1)S(1)} all-to-all(bf16[4,32,896]{2,1,0:T(8,128)(2,1)S(1)} %bitcast.83), channel_id=1, replica_groups=mesh['groups'=2,'ctx'=4,'exp'=2,'head'=2] {'ctx'}, dimensions={0} | all-to-all | bytes 458752 | tf_op jit(solution)/shard_map/all_to_all | solution.py:119
  137.7 0.1 copy.56
  137.9 0.1 reshape.91
  137.9 8.0 %all_to_all.36 = bf16[4,8,3584]{2,1,0:T(8,128)(2,1)S(1)} all-to-all(bf16[4,8,3584]{2,1,0:T(8,128)(2,1)S(1)} %reshape.91), channel_id=1, replica_groups=mesh['groups'=2,'ctx'=4,'exp'=2,'head'=2] {'exp','head'}, dimensions={0} | all-to-all | bytes 458752 | tf_op jit(solution)/shard_map/all_to_all | solution.py:126
  146.0 0.8 fusion.2
  (9 shorter events, 0.1 us)
Async XLA Ops:
  6.5 41.6 %copy-start = (bf16[512,896]{1,0:T(8,128)(2,1)S(1)}, bf16[512,896]{1,0:T(8,128)(2,1)}, u32[]{:S(2)}) copy-start(bf16[512,896]{1,0:T(8,128)(2,1)} %param.16) | copy-start | bytes 2752516
  6.5 61.1 %reduce-scatter.4.cloned.1.call-start = ((), (), s32[]{:S(2)}) async-start(), calls=%async_computation.5 | async-start | bytes 286720
  7.5 9.0 %collective-permute-start = (bf16[32,576]{0,1:T(8,128)(2,1)S(1)}, bf16[32,576]{0,1:T(8,128)(2,1)S(1)}, u32[]{:S(2)}, u32[]{:S(2)}) collective-permute-start(bf16[32,576]{0,1:T(8,128)(2,1)S(1)} %copy.45), channel_id=1, source_target_pairs={{0,4},{4,8},{8,12},{12,0},{1,5},{5,9},{9,13},{13,1},{2,6},{6,10},{... | collective-permute-start | bytes 110600 | tf_op jit(solution)/shard_map/ppermute | solution.py:39
  16.5 6.9 %collective-permute-start.1 = (bf16[32,576]{0,1:T(8,128)(2,1)S(1)}, bf16[32,576]{0,1:T(8,128)(2,1)S(1)}, u32[]{:S(2)}, u32[]{:S(2)}) collective-permute-start(bf16[32,576]{0,1:T(8,128)(2,1)S(1)} %collective-permute-done), channel_id=1, source_target_pairs={{0,4},{4,8},{8,12},{12,0},{1,5},{5,9},{9,13},{13,1},{2,6},{6,10},{... | collective-permute-start | bytes 110600 | tf_op jit(solution)/shard_map/ppermute | solution.py:39
  23.5 6.9 %collective-permute-start.2 = (bf16[32,576]{0,1:T(8,128)(2,1)S(1)}, bf16[32,576]{0,1:T(8,128)(2,1)S(1)}, u32[]{:S(2)}, u32[]{:S(2)}) collective-permute-start(bf16[32,576]{0,1:T(8,128)(2,1)S(1)} %collective-permute-done.1), channel_id=1, source_target_pairs={{0,4},{4,8},{8,12},{12,0},{1,5},{5,9},{9,13},{13,1},{2,6},{6,10},{... | collective-permute-start | bytes 110600 | tf_op jit(solution)/shard_map/ppermute | solution.py:39
  23.5 50.2 %copy-start.4 = (f32[8,2]{0,1:T(2,128)S(1)}, f32[8,2]{0,1:T(2,128)}, u32[]{:S(2)}) copy-start(f32[8,2]{0,1:T(2,128)} %param.23) | copy-start | bytes 196
  24.5 55.0 %copy-start.2 = (bf16[8,3584]{1,0:T(8,128)(2,1)S(1)}, bf16[8,3584]{1,0:T(8,128)(2,1)}, u32[]{:S(2)}) copy-start(bf16[8,3584]{1,0:T(8,128)(2,1)} %param.17) | copy-start | bytes 172036
  25.4 54.3 %copy-start.3 = (f32[3584]{0:T(1024)S(1)}, f32[3584]{0:T(1024)}, u32[]{:S(2)}) copy-start(f32[3584]{0:T(1024)} %param.18) | copy-start | bytes 43012
  69.1 10.3 %all-to-all-start = ((bf16[4,8,896]{2,1,0:T(8,128)(2,1)}), bf16[4,8,896]{2,1,0:T(8,128)(2,1)S(1)}, u32[]{:S(2)}, u32[]{:S(2)}) async-start(bf16[4,8,896]{2,1,0:T(8,128)(2,1)} %copy.58), calls=%async_computation | async-start | bytes 114688 | tf_op jit(solution)/shard_map/all_to_all | solution.py:84
  79.5 30.4 %copy-start.5 = (bf16[1,3584,512]{2,1,0:T(8,128)(2,1)S(1)}, bf16[1,3584,512]{2,1,0:T(8,128)(2,1)}, u32[]{:S(2)}) copy-start(bf16[1,3584,512]{2,1,0:T(8,128)(2,1)} %param.20) | copy-start | bytes 11010052
  109.8 16.4 %copy-start.1 = (bf16[1,2048,896]{2,1,0:T(8,128)(2,1)S(1)}, bf16[1,2048,896]{2,1,0:T(8,128)(2,1)}, u32[]{:S(2)}) copy-start(bf16[1,2048,896]{2,1,0:T(8,128)(2,1)} %param.21) | copy-start | bytes 11010052
Sparse Core Ops, SparseCore 0:
  49.4 18.1 reduce-scatter.3
